TPU v7x, 512 devices: a whole 4x8x8 slice. The times are simulated.
512 devices in a mesh: snode: 64 (over z, y), rows: 8 (over x, core).
Axes of the slice: x: 4, y: 8, z: 8, core: 2. Of those that a mesh axis runs over, the one named last changes fastest.
Arguments:
- anc_store: bfloat16 [8192, 8192], P('snode'), may hold values from -9 to 9
- patterns: int32 [64, 8], replicated, may hold values from 0 to 63, all different within a row
- tile_counts: int32 [64], replicated, may hold values from 1 to 8, 448 in all
- tile_owner: int32 [64], replicated, may hold values from 0 to 63, as said below
- l_offdiag: bfloat16 [65536, 512], P(('snode', 'rows')), may hold values from -0.25 to 0.25
- diag_inverse: bfloat16 [32768, 512], P(('snode', 'rows')), may hold values from -1 to 2, as said below
Outputs:
- sigma_offdiag: bfloat16 [65536, 512], P(('snode', 'rows'))
- sigma_diag: float32 [32768, 512], P(('snode', 'rows'))
Inputs may be any that keep to these rules, and one draw needn't show every extreme that they name: `patterns`: each supernode's row names 8 different ancestor tiles. Slots before tile_counts[s] of a supernode's pattern are live, the rest padding; some supernode has all 8 slots live. `tile_owner`: a permutation of the ancestor tiles. `diag_inverse`: each supernode's block of 512 rows is lower triangular with diagonal entries between 1 and 2.
All inputs are finite; a program needn't handle non-finite values.
Results may differ from a plain program's by a relative error of at most 0.014.
Values may be sent and summed in bfloat16 or wider, within the bound.
A program may use at most 64 MiB of HBM per device.

v0:
```python
import jax
import jax.numpy as jnp
from jax import lax
from jax.sharding import PartitionSpec as P


def row_block(matrix, index):
    return lax.dynamic_index_in_dim(matrix, index, 0, keepdims=False)


def per_device(anc_store, patterns, tile_counts, tile_owner, l_offdiag, diag_inverse):
    tile_rows = anc_store.shape[0]
    pool_size = tile_owner.shape[0]
    group_count = patterns.shape[0]
    pattern_len = patterns.shape[1]
    group_id = lax.axis_index("snode")
    part_id = lax.axis_index("rows")
    local_tiles = l_offdiag.shape[0] // tile_rows
    band_rows = diag_inverse.shape[0]
    band_start = part_id * band_rows
    live_mask = jnp.arange(pattern_len, dtype=jnp.int32)[None, :] < tile_counts[:, None]
    own_live = lax.dynamic_slice_in_dim(
        row_block(live_mask, group_id), part_id * local_tiles, local_tiles
    )
    keep_rows = jnp.repeat(own_live, tile_rows)
    masked_l = jnp.where(keep_rows[:, None], l_offdiag, jnp.zeros_like(l_offdiag))
    piece = lax.all_gather(diag_inverse, "rows", axis=0, tiled=True)
    u_total = jnp.dot(masked_l, piece, preferred_element_type=jnp.float32)
    own_cols = lax.dynamic_slice_in_dim(piece, band_start, band_rows, 1)
    d_total = lax.dot_general(
        own_cols, piece, (((0,), (0,)), ((), ())), preferred_element_type=jnp.float32
    )
    u_total, base_diag = (u_total, d_total)
    u_factor = u_total.astype(jnp.bfloat16)
    owned_tile = jnp.sum(
        jnp.arange(pool_size, dtype=jnp.int32) * (tile_owner == group_id).astype(jnp.int32)
    )
    send_flag = jnp.any((patterns == owned_tile) & live_mask, axis=1)
    own_pattern = row_block(patterns, group_id)
    sources = jnp.take(tile_owner, own_pattern, axis=0)
    col_tiles = lax.dynamic_slice_in_dim(patterns, part_id * local_tiles, local_tiles, 1)
    stored_blocks = anc_store.reshape(tile_rows, pool_size, tile_rows)
    picked = jnp.take(stored_blocks, col_tiles, axis=1)
    picked = jnp.transpose(picked, (1, 0, 2, 3)).reshape(
        group_count, tile_rows, local_tiles * tile_rows
    )
    outgoing = jnp.where(send_flag[:, None, None], picked, jnp.zeros_like(picked))
    incoming = lax.all_to_all(outgoing, "snode", split_axis=0, concat_axis=0, tiled=True)
    arranged = jnp.take(incoming, sources, axis=0).reshape(
        pattern_len * tile_rows, local_tiles * tile_rows
    )
    own_rows = lax.all_to_all(arranged, "rows", split_axis=0, concat_axis=1, tiled=True)
    y_block = jnp.dot(
        own_rows,
        lax.all_gather(u_factor, "rows", axis=0, tiled=True),
        preferred_element_type=jnp.float32,
    )
    offdiag = (-y_block).astype(jnp.bfloat16)
    partial_diag = lax.dot_general(
        u_factor, offdiag, (((0,), (0,)), ((), ())), preferred_element_type=jnp.float32
    )
    whole_update = lax.psum(partial_diag.astype(jnp.bfloat16), "rows").astype(jnp.float32)
    reduced = lax.dynamic_slice_in_dim(whole_update, band_start, band_rows, 0)
    return (offdiag, base_diag - reduced)


def solution(mesh):
    in_specs = (
        P("snode", None),
        P(),
        P(),
        P(),
        P(("snode", "rows"), None),
        P(("snode", "rows"), None),
    )
    out_specs = (P(("snode", "rows"), None), P(("snode", "rows"), None))
    return jax.shard_map(
        per_device, mesh=mesh, in_specs=in_specs, out_specs=out_specs, check_vma=False
    )
```

profile of v0, /device:TPU:1, one launch (start us, length us, event | category | flops | bytes accessed | tf_op | source)
XLA Modules:
  0.0 178.8 jit_solution(5158815995826037886)
XLA Ops:
  7.2 0.7 and_bitcast_fusion
  7.9 3.2 %copy.8 = bf16[128,8192]{0,1:T(8,128)(2,1)S(1)} copy(bf16[128,8192]{1,0:T(8,128)(2,1)} %param.6) | data formatting | bytes 4194304 | tf_op args[0]
  11.1 2.9 %copy.9 = bf16[128,64,128]{2,0,1:T(8,128)(2,1)} copy(bf16[128,64,128]{0,2,1:T(8,128)(2,1)S(1)} %bitcast.37) | data formatting | bytes 4194304 | tf_op jit(solution)/shard_map/reshape | solution.py:42
  14.0 0.0 copy-start
  14.0 0.0 copy-start.5
  14.0 0.0 copy-start.6
  14.0 2.6 %gather_fusion.1 = bf16[64,128,128]{2,1,0:T(8,128)(2,1)S(1)} fusion(bf16[128,64,128]{2,0,1:T(8,128)(2,1)} %copy.9, s32[1024]{0:T(1024)S(1)} %pad_clamp_fusion.1), kind=kCustom, calls=%fused_computation.1 | custom fusion | bytes 4194560 | tf_op jit(solution)/shard_map/jit(_take)/gather | solution.py:43
  16.6 0.0 copy-done
  16.6 0.6 fusion.6
  17.2 0.0 copy-done.5
  17.2 0.0 copy-done.6
  17.3 0.7 iota_compare_fusion
  17.9 1.7 bitcast_select_fusion
  19.6 0.0 copy-start.4
  19.6 0.0 copy-start.3
  19.6 17.3 %all-to-all-start = ((bf16[64,128,128]{2,1,0:T(8,128)(2,1)}), bf16[64,128,128]{2,1,0:T(8,128)(2,1)S(1)}, u32[]{:S(2)}, u32[]{:S(2)}) async-start(bf16[64,128,128]{2,1,0:T(8,128)(2,1)} %bitcast_select_fusion), calls=%async_computation | async-start | bytes 4194304 | tf_op jit(solution)/shard_map/all_to_all | solution.py:48
  36.9 0.0 all-gather.2.cloned.1.call-start
  36.9 0.6 dynamic_slice.22
  37.5 0.0 copy-done.4
  37.5 14.2 %all_gather.6 = bf16[512,512]{1,0:T(8,128)(2,1)S(1)} all-gather(bf16[64,512]{1,0:T(8,128)(2,1)S(1)} %copy-done.4), channel_id=1, replica_groups=mesh['snode'=64,'rows'=8] {'rows'}, dimensions={0}, use_global_device_ids=true | all-gather | bytes 589824 | tf_op jit(solution)/shard_map/all_gather | solution.py:27
  51.8 0.0 copy-done.3
  51.8 1.5 convolution_convert_fusion.1
  53.3 0.0 copy-start.1
  53.3 0.0 all-gather.2.cloned.1.call-update
  53.3 0.0 all-reduce.2.cloned.1.call-start
  53.4 0.2 dynamic-slice_reduce_fusion
  53.6 0.6 gather_fusion
  54.3 31.9 %all-to-all-done = bf16[64,128,128]{2,1,0:T(8,128)(2,1)S(1)} async-done(((bf16[64,128,128]{2,1,0:T(8,128)(2,1)}), bf16[64,128,128]{2,1,0:T(8,128)(2,1)S(1)}, u32[]{:S(2)}, u32[]{:S(2)}) %all-to-all-start) | async-done | bytes 2097184 | tf_op jit(solution)/shard_map/all_to_all | solution.py:48
  86.2 0.6 gather_fusion.2
  86.8 0.1 broadcast_select_fusion
  86.9 14.6 %all_to_all.21 = bf16[8,128,128]{2,1,0:T(8,128)(2,1)S(1)} all-to-all(bf16[8,128,128]{2,1,0:T(8,128)(2,1)S(1)} %broadcast_select_fusion), channel_id=1, replica_groups=mesh['snode'=64,'rows'=8] {'rows'}, dimensions={0} | all-to-all | bytes 524288 | tf_op jit(solution)/shard_map/all_to_all | solution.py:52
  101.5 0.2 copy.10
  101.7 0.0 all-gather.2.cloned.1.call-done
  101.7 1.6 fusion
  103.3 0.0 copy-done.1
  103.3 0.0 copy-start.2
  103.3 1.1 convolution_convert_fusion
  104.4 0.0 all-reduce.2.cloned.1.call-update
  104.4 65.7 %all-reduce.2.cloned.1.call-done = bf16[512,512]{1,0:T(8,128)(2,1)} async-done(((bf16[512,512]{1,0:T(8,128)(2,1)}), bf16[512,512]{1,0:T(8,128)(2,1)}) %all-reduce.2.cloned.1.call-update) | async-done | bytes 524304 | tf_op jit(solution)/shard_map/psum | solution.py:62
  170.1 1.8 %convolution_subtract_fusion = f32[64,512]{1,0:T(8,128)} fusion(bf16[512,512]{1,0:T(8,128)(2,1)S(1)} %all_gather.6, s32[]{:T(128)S(6)} %select_n.116, bf16[512,512]{1,0:T(8,128)(2,1)} %all-reduce.2.cloned.1.call-done), kind=kOutput, calls=%fused_computation.9 | convolution fusion | flops 33619968 | bytes 852992 | tf_op jit(solution)/shard_map/dot_general | solution.py:30
  171.9 0.0 copy-done.2
  (6 shorter events, 0.0 us)
Async XLA Ops:
  14.0 2.6 %copy-start = (s32[64]{0:T(128)S(1)}, s32[64]{0:T(128)}, u32[]{:S(2)}) copy-start(s32[64]{0:T(128)} %param.9) | copy-start | bytes 772
  14.0 3.2 %copy-start.5 = (s32[64,8]{0,1:T(8,128)S(1)}, s32[64,8]{0,1:T(8,128)}, u32[]{:S(2)}) copy-start(s32[64,8]{0,1:T(8,128)} %param.7) | copy-start | bytes 6148
  14.0 3.2 %copy-start.6 = (s32[64]{0:T(128)S(1)}, s32[64]{0:T(128)}, u32[]{:S(2)}) copy-start(s32[64]{0:T(128)} %param.8) | copy-start | bytes 772
  19.6 17.9 %copy-start.4 = (bf16[64,512]{1,0:T(8,128)(2,1)S(1)}, bf16[64,512]{1,0:T(8,128)(2,1)}, u32[]{:S(2)}) copy-start(bf16[64,512]{1,0:T(8,128)(2,1)} %param.11) | copy-start | bytes 196612
  19.6 32.2 %copy-start.3 = (bf16[128,512]{1,0:T(8,128)(2,1)S(1)}, bf16[128,512]{1,0:T(8,128)(2,1)}, u32[]{:S(2)}) copy-start(bf16[128,512]{1,0:T(8,128)(2,1)} %param.10) | copy-start | bytes 393220
  19.6 66.6 %all-to-all-start = ((bf16[64,128,128]{2,1,0:T(8,128)(2,1)}), bf16[64,128,128]{2,1,0:T(8,128)(2,1)S(1)}, u32[]{:S(2)}, u32[]{:S(2)}) async-start(bf16[64,128,128]{2,1,0:T(8,128)(2,1)} %bitcast_select_fusion), calls=%async_computation | async-start | bytes 4194304 | tf_op jit(solution)/shard_map/all_to_all | solution.py:48
  36.9 64.8 %all-gather.2.cloned.1.call-start = ((), (), s32[]{:S(2)}) async-start(), calls=%async_computation.2 | async-start | bytes 1179648 | tf_op jit(solution)/shard_map/all_gather | solution.py:55
  53.3 50.0 %copy-start.1 = (bf16[128,512]{1,0:T(8,128)(2,1)S(1)}, bf16[128,512]{1,0:T(8,128)(2,1)}, u32[]{:S(2)}) copy-start(bf16[128,512]{1,0:T(8,128)(2,1)} %convolution_convert_fusion.1) | copy-start | bytes 393220
  53.3 116.8 %all-reduce.2.cloned.1.call-start = ((), (), s32[]{:S(2)}) async-start(), calls=%async_computation.3 | async-start | bytes 1048576 | tf_op jit(solution)/shard_map/psum | solution.py:62
  103.3 68.6 %copy-start.2 = (bf16[128,512]{1,0:T(8,128)(2,1)}, bf16[128,512]{1,0:T(8,128)(2,1)S(1)}, u32[]{:S(2)}) copy-start(bf16[128,512]{1,0:T(8,128)(2,1)S(1)} %fusion) | copy-start | bytes 393220
Sparse Core Ops, SparseCore 0:
  53.4 28.7 all-gather.1
  104.6 65.5 all-reduce.1
where the time goes:
time: 180 us; the launch traced here: 179 us
  waiting for transfers between devices  97.6 us (54%)
  blocking collectives  28.9 us (16%)
  starting transfers between devices  17.4 us (10%)
  between operations  14.2 us (8%)
  local copies, waits for them, and re-layouts  10.9 us (6%)
  matrix products  6 us (3%)
  other arithmetic  3.82 us (2%)
    psum x1, waiting for transfers between devices, per_device(): lax.psum(partial_diag.astype(jnp.bfloat16), 'rows').astype(jnp.float32)  65.7 us
    all_to_all x1, waiting for transfers between devices, per_device(): lax.all_to_all(outgoing, 'snode', split_axis=0, concat_axis=0, tiled=True)  31.9 us
    all_to_all x1, starting transfers between devices, per_device(): lax.all_to_all(outgoing, 'snode', split_axis=0, concat_axis=0, tiled=True)  17.3 us
    all_to_all x1, blocking collectives, per_device(): lax.all_to_all(arranged, 'rows', split_axis=0, concat_axis=1, tiled=True)  14.6 us
    all_gather x1, blocking collectives, per_device(): piece = lax.all_gather(diag_inverse, 'rows', axis=0, tiled=True)  14.2 us
  transfers between devices with their start and end apart: 3, of which 2 were waited for; matrix products, arithmetic and copies ran while one was open for 2% of the time, Pallas kernels for 0%

commit v1 on v0

v1 whole, which is shorter than its diff:
```python
import functools

import jax
import jax.numpy as jnp
from jax import lax
from jax.experimental import pallas as pl
from jax.experimental.pallas import tpu as pltpu
from jax.sharding import PartitionSpec as P

MESH = pl.DeviceIdType.MESH
VMEM = pl.BlockSpec(memory_space=pltpu.VMEM)


def pick_kernel(count, tile, cols_ref, store_ref, out_ref, sem):
    def start(i, carry):
        col = pl.multiple_of(cols_ref[i] * tile, tile)
        pltpu.make_async_copy(store_ref.at[:, pl.ds(col, tile)], out_ref.at[i], sem).start()
        return carry

    lax.fori_loop(0, count, start, 0)
    pltpu.make_async_copy(out_ref, out_ref, sem).wait()


def pick_tiles(store, cols, tile):
    count = cols.shape[0]
    return pl.pallas_call(
        functools.partial(pick_kernel, count, tile),
        out_shape=jax.ShapeDtypeStruct((count, store.shape[0], tile), store.dtype),
        in_specs=[pl.BlockSpec(memory_space=pltpu.SMEM), pl.BlockSpec(memory_space=pl.ANY)],
        out_specs=VMEM,
        scratch_shapes=[pltpu.SemaphoreType.DMA],
        name="pick_tiles",
    )(cols, store)


def greet(n):
    snode, me = lax.axis_index("snode"), lax.axis_index("rows")
    barrier = pltpu.get_barrier_semaphore()
    for step in range(1, n):
        pl.semaphore_signal(
            barrier, inc=1, device_id=(snode, lax.rem(me + step, n)), device_id_type=MESH
        )
    pl.semaphore_wait(barrier, n - 1)


def exchange(n, gather, src_ref, dst_ref, send_sem, recv_sem, local_sem):
    snode, me = lax.axis_index("snode"), lax.axis_index("rows")
    greet(n)
    copies = []
    for step in range(1, n):
        peer = lax.rem(me + step, n)
        copy = pltpu.make_async_remote_copy(
            src_ref=src_ref if gather else src_ref.at[peer],
            dst_ref=dst_ref.at[me],
            send_sem=send_sem.at[step - 1],
            recv_sem=recv_sem.at[step - 1],
            device_id=(snode, peer),
            device_id_type=MESH,
        )
        copy.start()
        copies.append(copy)
    own = pltpu.make_async_copy(
        src_ref if gather else src_ref.at[me], dst_ref.at[me], local_sem
    )
    own.start()
    own.wait()
    for copy in copies:
        copy.wait()


def sems(n):
    return [
        pltpu.SemaphoreType.DMA((n - 1,)),
        pltpu.SemaphoreType.DMA((n - 1,)),
        pltpu.SemaphoreType.DMA,
    ]


def gather_kernel(n, x_ref, o_ref, *semaphores):
    exchange(n, True, x_ref, o_ref, *semaphores)


def gather_rows(x, n, collective_id, name):
    return pl.pallas_call(
        functools.partial(gather_kernel, n),
        out_shape=jax.ShapeDtypeStruct((n,) + x.shape, x.dtype),
        in_specs=[VMEM],
        out_specs=VMEM,
        scratch_shapes=sems(n),
        compiler_params=pltpu.CompilerParams(collective_id=collective_id, has_side_effects=True),
        name=name,
    )(x)


def product_kernel(n, tiles_ref, u_ref, own_u_ref, live_ref, y_ref, part_ref, held, *semaphores):
    exchange(n, False, tiles_ref, held, *semaphores)
    total = jnp.zeros(y_ref.shape, jnp.float32)
    for m in range(n):
        total += jnp.dot(held[m], u_ref[m], preferred_element_type=jnp.float32)
    y = (-(total * live_ref[...])).astype(y_ref.dtype)
    y_ref[...] = y
    part = lax.dot_general(
        own_u_ref[...], y, (((0,), (0,)), ((), ())), preferred_element_type=jnp.float32
    )
    part_ref[...] = part.astype(part_ref.dtype).reshape(part_ref.shape)


def product(tiles, u_all, own_u, live, n, collective_id):
    width = own_u.shape[1]
    return pl.pallas_call(
        functools.partial(product_kernel, n),
        out_shape=(
            jax.ShapeDtypeStruct(own_u.shape, jnp.bfloat16),
            jax.ShapeDtypeStruct((n, width // n, width), jnp.bfloat16),
        ),
        in_specs=[VMEM] * 4,
        out_specs=(VMEM, VMEM),
        scratch_shapes=[pltpu.VMEM(tiles.shape, tiles.dtype)] + sems(n),
        compiler_params=pltpu.CompilerParams(collective_id=collective_id, has_side_effects=True),
        name="product",
    )(tiles, u_all, own_u, live)


def update_kernel(n, part_ref, base_ref, o_ref, held, *semaphores):
    exchange(n, False, part_ref, held, *semaphores)
    total = base_ref[...]
    for m in range(n):
        total -= held[m].astype(jnp.float32)
    o_ref[...] = total


def update(part, base, n, collective_id):
    return pl.pallas_call(
        functools.partial(update_kernel, n),
        out_shape=jax.ShapeDtypeStruct(base.shape, jnp.float32),
        in_specs=[VMEM] * 2,
        out_specs=VMEM,
        scratch_shapes=[pltpu.VMEM(part.shape, part.dtype)] + sems(n),
        compiler_params=pltpu.CompilerParams(collective_id=collective_id, has_side_effects=True),
        name="update",
    )(part, base)


def per_device(n, anc_store, patterns, tile_counts, tile_owner, l_offdiag, diag_inverse):
    tile = anc_store.shape[0]
    width = diag_inverse.shape[1]
    band = diag_inverse.shape[0]
    group = lax.axis_index("snode")
    part = lax.axis_index("rows")
    cols = lax.dynamic_slice_in_dim(patterns, part, 1, 1)[:, 0]
    outgoing = pick_tiles(anc_store, cols, tile)
    incoming = lax.all_to_all(outgoing, "snode", split_axis=0, concat_axis=0, tiled=True)

    own_live = part < lax.dynamic_index_in_dim(tile_counts, group, 0, keepdims=False)
    piece = gather_rows(diag_inverse, n, 1, "gather_diag").reshape(width, width)
    masked_l = jnp.where(own_live, l_offdiag, jnp.zeros_like(l_offdiag))
    own_u = jnp.dot(masked_l, piece, preferred_element_type=jnp.float32).astype(jnp.bfloat16)
    u_all = gather_rows(own_u, n, 2, "gather_u")
    own_cols = lax.dynamic_slice_in_dim(piece, part * band, band, 1)
    base = lax.dot_general(
        own_cols, piece, (((0,), (0,)), ((), ())), preferred_element_type=jnp.float32
    )

    own_pattern = lax.dynamic_index_in_dim(patterns, group, 0, keepdims=False)
    sources = jnp.take(tile_owner, own_pattern, axis=0, mode="clip")
    arranged = jnp.take(incoming, sources, axis=0, mode="clip")
    live = jnp.broadcast_to(own_live.astype(jnp.float32), (1, width))
    offdiag, parts = product(arranged, u_all, own_u, live, n, 3)
    return offdiag, update(parts, base, n, 4)


def solution(mesh):
    in_specs = (
        P("snode", None),
        P(),
        P(),
        P(),
        P(("snode", "rows"), None),
        P(("snode", "rows"), None),
    )
    out_specs = (P(("snode", "rows"), None), P(("snode", "rows"), None))
    return jax.shard_map(
        functools.partial(per_device, mesh.shape["rows"]),
        mesh=mesh,
        in_specs=in_specs,
        out_specs=out_specs,
        check_vma=False,
    )
```

time: 180 us -> 109 us (0.61)
  the two profiles are of different devices: /device:TPU:1 before, /device:TPU:25 now
where the time goes in v1:
time: 109 us; the launch traced here: 108 us
  Pallas kernels  60.6 us (56%)
  waiting for transfers between devices  19.5 us (18%)
  starting transfers between devices  15.9 us (15%)
  local copies, waits for them, and re-layouts  7.62 us (7%)
  matrix products  2.95 us (3%)
  between operations  1.42 us (1%)
    pallas_call x2, Pallas kernels, gather_rows(): pl.pallas_call(functools.partial(gather_kernel, n), out_shape=jax.ShapeDt...  31.7 us
    all_to_all x1, waiting for transfers between devices, per_device(): lax.all_to_all(outgoing, 'snode', split_axis=0, concat_axis=0, tiled=True)  19.5 us
    all_to_all x1, starting transfers between devices, per_device(): lax.all_to_all(outgoing, 'snode', split_axis=0, concat_axis=0, tiled=True)  15.9 us
    pallas_call x1, Pallas kernels, update(): pl.pallas_call(functools.partial(update_kernel, n), out_shape=jax.ShapeDt...  12.4 us
    pallas_call x1, Pallas kernels, product(): pl.pallas_call(functools.partial(product_kernel, n), out_shape=(jax.Shape...  12 us
    pallas_call x1, Pallas kernels, pick_tiles(): pl.pallas_call(functools.partial(pick_kernel, count, tile), out_shape=jax...  4.45 us
    unnamed x12, local copies, waits for them, and re-layouts  3.84 us
  transfers between devices with their start and end apart: 1, of which 1 were waited for; matrix products, arithmetic and copies ran while one was open for 4% of the time, Pallas kernels for 29%

profile of v1, /device:TPU:25, one launch (start us, length us, event | category | flops | bytes accessed | tf_op | source)
XLA Modules:
  0.0 108.0 jit_solution(13492553048899856151)
XLA Ops:
  0.6 0.0 copy-start
  0.6 0.7 copy-done
  1.3 0.5 fusion.6.cols_ref
  1.8 4.4 %pick_tiles.1 = bf16[64,128,128]{2,1,0:T(8,128)(2,1)} custom-call(s32[64]{0:T(128)} %fusion.6.cols_ref, bf16[128,8192]{1,0:T(8,128)(2,1)} %store_ref.1), custom_call_target="tpu_custom_call" | custom-call | tf_op jit(solution)/shard_map/pick_tiles/pallas_call | solution.py:26
  6.3 0.0 copy-start.4
  6.3 0.0 copy-start.3
  6.3 15.9 %all-to-all-start = ((bf16[64,128,128]{2,1,0:T(8,128)(2,1)}), bf16[64,128,128]{2,1,0:T(8,128)(2,1)S(1)}, u32[]{:S(2)}, u32[]{:S(2)}) async-start(bf16[64,128,128]{2,1,0:T(8,128)(2,1)} %pick_tiles.1), calls=%async_computation | async-start | bytes 4194304 | tf_op jit(solution)/shard_map/all_to_all | solution.py:152
  22.3 0.0 copy-start.1
  22.3 0.2 dynamic-slice_reduce_fusion
  22.5 0.0 copy-done.4
  22.5 0.6 dynamic_slice.16
  23.7 13.5 %gather_diag.1 = bf16[8,64,512]{2,1,0:T(8,128)(2,1)} custom-call(bf16[64,512]{1,0:T(8,128)(2,1)} %x_ref.1), custom_call_target="tpu_custom_call" | custom-call | tf_op jit(solution)/shard_map/gather_diag/pallas_call | solution.py:84
  37.2 0.0 copy-start.2
  37.2 0.0 copy-done.3
  37.2 2.0 %convolution_convert_fusion.x_ref.own_u_ref = bf16[128,512]{1,0:T(8,128)(2,1)} fusion(bf16[512,512]{1,0:T(8,128)(2,1)} %bitcast.6, bf16[128,512]{1,0:T(8,128)(2,1)S(1)} %copy-done.3, pred[]{:T(512)S(6)} %lt.17), kind=kOutput, calls=%fused_computation.2 | convolution fusion | flops 67239936 | bytes 786433 | tf_op jit(solution)/shard_map/dot_general | solution.py:157
  39.2 18.2 %gather_u.1.u_ref = bf16[8,128,512]{2,1,0:T(8,128)(2,1)} custom-call(bf16[128,512]{1,0:T(8,128)(2,1)} %convolution_convert_fusion.x_ref.own_u_ref), custom_call_target="tpu_custom_call" | custom-call | tf_op jit(solution)/shard_map/gather_u/pallas_call | solution.py:84
  57.5 0.0 copy-done.1
  57.5 0.6 gather_fusion
  58.1 0.0 copy-done.2
  58.1 1.0 fusion.base_ref
  59.1 19.5 %all-to-all-done = bf16[64,128,128]{2,1,0:T(8,128)(2,1)S(1)} async-done(((bf16[64,128,128]{2,1,0:T(8,128)(2,1)}), bf16[64,128,128]{2,1,0:T(8,128)(2,1)S(1)}, u32[]{:S(2)}, u32[]{:S(2)}) %all-to-all-start) | async-done | bytes 2097184 | tf_op jit(solution)/shard_map/all_to_all | solution.py:152
  78.6 1.3 %gather_fusion.1 = bf16[8,128,128]{2,1,0:T(8,128)(2,1)} fusion(bf16[64,128,128]{2,1,0:T(8,128)(2,1)S(1)} %all-to-all-done, s32[1024]{0:T(1024)S(1)} %pad_clamp_fusion), kind=kCustom, calls=%fused_computation.1 | custom fusion | bytes 524320 | tf_op jit(solution)/shard_map/jit(_take)/gather | solution.py:166
  79.8 0.6 broadcast_in_dim.17.live_ref
  80.4 12.0 %product.1 = (bf16[128,512]{1,0:T(8,128)(2,1)}, bf16[8,64,512]{2,1,0:T(8,128)(2,1)}) custom-call(bf16[8,128,128]{2,1,0:T(8,128)(2,1)} %gather_fusion.1, bf16[8,128,512]{2,1,0:T(8,128)(2,1)} %gather_u.1.u_ref, bf16[128,512]{1,0:T(8,128)(2,1)} %convolution_convert_fusion.x_ref.own_u_ref, f32[1,512]{1,0:T(1,128)} %broadcast_in_dim.17.live_ref), custom_call_target="tpu_custom_call" | custom-call | tf_op jit(solution)/shard_map/product/pallas_call | solution.py:110
  92.5 12.4 %update.1 = f32[64,512]{1,0:T(8,128)} custom-call(bf16[8,64,512]{2,1,0:T(8,128)(2,1)} %get-tuple-element.5.part_ref, f32[64,512]{1,0:T(8,128)} %fusion.base_ref), custom_call_target="tpu_custom_call" | custom-call | tf_op jit(solution)/shard_map/update/pallas_call | solution.py:133
  104.9 1.6 %copy.10 = bf16[128,512]{1,0:T(8,128)(2,1)} copy(bf16[128,512]{1,0:T(8,128)(2,1)} %get-tuple-element.8) | data formatting | bytes 262144
  106.4 1.6 %copy.11 = f32[64,512]{1,0:T(8,128)} copy(f32[64,512]{1,0:T(8,128)} %update.1) | data formatting | bytes 262144
  (2 shorter events, 0.0 us)
Async XLA Ops:
  0.6 0.7 copy-start
  6.3 16.2 %copy-start.4 = (s32[64]{0:T(128)S(1)}, s32[64]{0:T(128)}, u32[]{:S(2)}) copy-start(s32[64]{0:T(128)} %param.8) | copy-start | bytes 772
  6.3 30.9 %copy-start.3 = (bf16[128,512]{1,0:T(8,128)(2,1)S(1)}, bf16[128,512]{1,0:T(8,128)(2,1)}, u32[]{:S(2)}) copy-start(bf16[128,512]{1,0:T(8,128)(2,1)} %param.10) | copy-start | bytes 393220
  6.3 72.2 %all-to-all-start = ((bf16[64,128,128]{2,1,0:T(8,128)(2,1)}), bf16[64,128,128]{2,1,0:T(8,128)(2,1)S(1)}, u32[]{:S(2)}, u32[]{:S(2)}) async-start(bf16[64,128,128]{2,1,0:T(8,128)(2,1)} %pick_tiles.1), calls=%async_computation | async-start | bytes 4194304 | tf_op jit(solution)/shard_map/all_to_all | solution.py:152
  22.3 35.2 %copy-start.1 = (s32[64]{0:T(128)S(1)}, s32[64]{0:T(128)}, u32[]{:S(2)}) copy-start(s32[64]{0:T(128)} %param.9) | copy-start | bytes 772
  37.2 20.9 %copy-start.2 = (bf16[8,64,512]{2,1,0:T(8,128)(2,1)S(1)}, bf16[8,64,512]{2,1,0:T(8,128)(2,1)}, u32[]{:S(2)}) copy-start(bf16[8,64,512]{2,1,0:T(8,128)(2,1)} %gather_diag.1) | copy-start | bytes 1572868

commit v2 on v1

v2 whole, which is shorter than its diff:
```python
import functools

import jax
import jax.numpy as jnp
from jax import lax
from jax.experimental import pallas as pl
from jax.experimental.pallas import tpu as pltpu
from jax.sharding import PartitionSpec as P

LANES = 128
MESH = pl.DeviceIdType.MESH
VMEM = pl.BlockSpec(memory_space=pltpu.VMEM)


def pick_kernel(count, tile, cols_ref, store_ref, out_ref, sem):
    def start(i, carry):
        col = pl.multiple_of(cols_ref[i] * tile, tile)
        pltpu.make_async_copy(store_ref.at[:, pl.ds(col, tile)], out_ref.at[i], sem).start()
        return carry

    lax.fori_loop(0, count, start, 0)
    pltpu.make_async_copy(out_ref, out_ref, sem).wait()


def pick_tiles(store, cols, tile):
    count = cols.shape[0]
    return pl.pallas_call(
        functools.partial(pick_kernel, count, tile),
        out_shape=jax.ShapeDtypeStruct((count, store.shape[0], tile), store.dtype),
        in_specs=[pl.BlockSpec(memory_space=pltpu.SMEM), pl.BlockSpec(memory_space=pl.ANY)],
        out_specs=VMEM,
        scratch_shapes=[pltpu.SemaphoreType.DMA],
        name="pick_tiles",
    )(cols, store)


def level_kernel(
    n, count, side,
    src_ref, out_tiles, l_ref, diag_ref, live_ref,
    y_ref, parts_ref, base_ref,
    pool, diag_all, u_all, stage, tiles, parts, wide, total,
    pool_send, pool_recv, row_send, row_recv, local_sem,
):
    snode, me = lax.axis_index("snode"), lax.axis_index("rows")
    major, minor = snode // side, lax.rem(snode, side)

    def other(step):
        shift = lax.rem(step * 27, count)
        to_major = lax.rem(major + shift // side, count // side)
        to_minor = lax.rem(minor + lax.rem(shift, side), side)
        return to_major * side + to_minor

    def greet_other(step, carry):
        pl.semaphore_signal(barrier, inc=1, device_id=(other(step), me), device_id_type=MESH)
        return carry

    barrier = pltpu.get_barrier_semaphore()
    for step in range(1, n):
        pl.semaphore_signal(
            barrier, inc=1, device_id=(snode, lax.rem(me + step, n)), device_id_type=MESH
        )
    lax.fori_loop(1, count, greet_other, 0)
    pl.semaphore_wait(barrier, n + count - 2)

    def row_copies(phase, src_of, dst):
        copies = []
        for step in range(1, n):
            peer = lax.rem(me + step, n)
            copy = pltpu.make_async_remote_copy(
                src_ref=src_of(peer),
                dst_ref=dst.at[me],
                send_sem=row_send.at[phase, step - 1],
                recv_sem=row_recv.at[phase, step - 1],
                device_id=(snode, peer),
                device_id_type=MESH,
            )
            copy.start()
            copies.append(copy)
        return copies

    def pool_copy(step):
        peer = other(step)
        return pltpu.make_async_remote_copy(
            src_ref=out_tiles.at[peer],
            dst_ref=pool.at[snode],
            send_sem=pool_send.at[step],
            recv_sem=pool_recv.at[step],
            device_id=(peer, me),
            device_id_type=MESH,
        )

    def start_pool(step, carry):
        pool_copy(step).start()
        return carry

    def wait_pool(step, carry):
        pool_copy(step).wait()
        return carry

    diag_copies = row_copies(0, lambda peer: diag_ref, diag_all)
    lax.fori_loop(1, count, start_pool, 0)
    own_diag = pltpu.make_async_copy(diag_ref, diag_all.at[me], local_sem.at[0])
    own_diag.start()
    own_tile = pltpu.make_async_copy(out_tiles.at[snode], pool.at[snode], local_sem.at[1])
    own_tile.start()
    own_diag.wait()
    for copy in diag_copies:
        copy.wait()

    band, width = diag_ref.shape
    depth = l_ref.shape[0]
    piece = diag_all[...].reshape(width, width)
    u_all[me] = jnp.dot(l_ref[...], piece, preferred_element_type=jnp.float32).astype(u_all.dtype)
    per_block = LANES // band
    start = pl.multiple_of(me // per_block * LANES, LANES)
    columns = diag_all[:, :, pl.ds(start, LANES)].reshape(width, LANES)
    wide[...] = lax.dot_general(
        columns, piece, (((0,), (0,)), ((), ())), preferred_element_type=jnp.float32
    )
    row = pl.multiple_of(lax.rem(me, per_block) * band, band)
    base_ref[...] = wide[pl.ds(row, band), :]
    u_copies = row_copies(1, lambda peer: u_all.at[me], u_all)
    for copy in u_copies:
        copy.wait()
    own_tile.wait()
    lax.fori_loop(1, count, wait_pool, 0)

    for k in range(n):
        stage[k] = pool[src_ref[k]]
    tile_copies = row_copies(2, lambda peer: stage.at[peer], tiles)
    total[...] = jnp.dot(stage[me], u_all[me], preferred_element_type=jnp.float32)
    for step, copy in enumerate(tile_copies):
        copy.wait()
        origin = lax.rem(me + n - 1 - step, n)
        total[...] += jnp.dot(tiles[origin], u_all[origin], preferred_element_type=jnp.float32)
    y = (-(total[...] * live_ref[...])).astype(y_ref.dtype)
    part = lax.dot_general(
        u_all[me], y, (((0,), (0,)), ((), ())), preferred_element_type=jnp.float32
    )
    parts[...] = part.astype(parts.dtype).reshape(parts.shape)
    y_ref[...] = y
    part_copies = row_copies(3, lambda peer: parts.at[peer], parts_ref)
    own_part = pltpu.make_async_copy(parts.at[me], parts_ref.at[me], local_sem.at[2])
    own_part.start()
    own_part.wait()
    for copy in part_copies:
        copy.wait()


def level(sources, outgoing, masked_l, diag, live, n, side):
    count, tile, _ = outgoing.shape
    band, width = diag.shape
    bf16 = jnp.bfloat16
    return pl.pallas_call(
        functools.partial(level_kernel, n, count, side),
        out_shape=(
            jax.ShapeDtypeStruct((tile, width), bf16),
            jax.ShapeDtypeStruct((n, band, width), bf16),
            jax.ShapeDtypeStruct((band, width), jnp.float32),
        ),
        in_specs=[pl.BlockSpec(memory_space=pltpu.SMEM)] + [VMEM] * 4,
        out_specs=(VMEM,) * 3,
        scratch_shapes=[
            pltpu.VMEM((count, tile, tile), bf16),
            pltpu.VMEM((n, band, width), bf16),
            pltpu.VMEM((n, tile, width), bf16),
            pltpu.VMEM((n, tile, tile), bf16),
            pltpu.VMEM((n, tile, tile), bf16),
            pltpu.VMEM((n, band, width), bf16),
            pltpu.VMEM((LANES, width), jnp.float32),
            pltpu.VMEM((tile, width), jnp.float32),
            pltpu.SemaphoreType.DMA((count,)),
            pltpu.SemaphoreType.DMA((count,)),
            pltpu.SemaphoreType.DMA((4, n - 1)),
            pltpu.SemaphoreType.DMA((4, n - 1)),
            pltpu.SemaphoreType.DMA((3,)),
        ],
        compiler_params=pltpu.CompilerParams(collective_id=1, has_side_effects=True),
        name="level",
    )(sources, outgoing, masked_l, diag, live)


def finish_kernel(y_ref, parts_ref, base_ref, off_ref, diag_ref):
    off_ref[...] = y_ref[...]
    total = base_ref[...]
    for m in range(parts_ref.shape[0]):
        total -= parts_ref[m].astype(jnp.float32)
    diag_ref[...] = total


def finish(y, parts, base):
    return pl.pallas_call(
        finish_kernel,
        out_shape=(
            jax.ShapeDtypeStruct(y.shape, y.dtype),
            jax.ShapeDtypeStruct(base.shape, base.dtype),
        ),
        in_specs=[VMEM] * 3,
        out_specs=(VMEM, VMEM),
        name="finish",
    )(y, parts, base)


def per_device(n, side, anc_store, patterns, tile_counts, tile_owner, l_offdiag, diag_inverse):
    tile = anc_store.shape[0]
    width = diag_inverse.shape[1]
    group = lax.axis_index("snode")
    part = lax.axis_index("rows")
    cols = lax.dynamic_slice_in_dim(patterns, part, 1, 1)[:, 0]
    outgoing = pick_tiles(anc_store, cols, tile)
    own_live = part < lax.dynamic_index_in_dim(tile_counts, group, 0, keepdims=False)
    masked_l = jnp.where(own_live, l_offdiag, jnp.zeros_like(l_offdiag))
    own_pattern = lax.dynamic_index_in_dim(patterns, group, 0, keepdims=False)
    pool_ids = jnp.arange(tile_owner.shape[0], dtype=jnp.int32)
    hit = own_pattern[:, None] == pool_ids[None, :]
    sources = jnp.sum(jnp.where(hit, tile_owner[None, :], 0), axis=1)
    live = jnp.broadcast_to(own_live.astype(jnp.float32), (1, width))
    return finish(*level(sources, outgoing, masked_l, diag_inverse, live, n, side))


def solution(mesh):
    in_specs = (
        P("snode", None),
        P(),
        P(),
        P(),
        P(("snode", "rows"), None),
        P(("snode", "rows"), None),
    )
    out_specs = (P(("snode", "rows"), None), P(("snode", "rows"), None))
    return jax.shard_map(
        functools.partial(per_device, mesh.shape["rows"], 8),
        mesh=mesh,
        in_specs=in_specs,
        out_specs=out_specs,
        check_vma=False,
    )
```

time: 109 us -> 97.8 us (0.90)
  the two profiles are of different devices: /device:TPU:25 before, /device:TPU:1 now
where the time goes in v2:
time: 97.8 us; the launch traced here: 97.4 us
  Pallas kernels  89.9 us (92%)
  local copies, waits for them, and re-layouts  3.21 us (3%)
  other arithmetic  2.98 us (3%)
  between operations  1.32 us (1%)
    pallas_call x1, Pallas kernels, level(): pl.pallas_call(functools.partial(level_kernel, n, count, side), out_shape...  84.1 us
    pallas_call x1, Pallas kernels, pick_tiles(): pl.pallas_call(functools.partial(pick_kernel, count, tile), out_shape=jax...  3.96 us

profile of v2, /device:TPU:1, one launch (start us, length us, event | category | flops | bytes accessed | tf_op | source)
XLA Modules:
  0.0 97.4 jit_solution(8812836135097841469)
XLA Ops:
  0.6 0.0 copy-start
  0.6 0.7 copy-done
  1.3 0.5 dynamic-slice_bitcast_fusion.cols_ref
  1.8 1.2 %dynamic_slice.13 = s32[1]{0:T(128)} dynamic-slice(s32[64]{0:T(128)} %param.8, s32[]{:T(128)S(6)} %select_n.21), dynamic_slice_sizes={1} | dynamic-slice | bytes 12 | tf_op jit(solution)/shard_map/jit(dynamic_index_in_dim)/dynamic_slice | solution.py:211
  3.7 0.2 dynamic-slice_reduce_fusion
  3.9 1.4 %select_reduce_fusion.src_ref = s32[8]{0:T(128)} fusion(s32[64]{0:T(128)} %param.9, s32[8]{0:T(128)S(1)} %dynamic-slice_reduce_fusion), kind=kLoop, calls=%fused_computation.1 | loop fusion | flops 1528 | bytes 320 | tf_op jit(solution)/shard_map/reduce_sum | solution.py:216
  5.3 0.6 broadcast_in_dim.24.live_ref
  5.9 1.6 %broadcast_select_fusion.l_ref = bf16[128,512]{1,0:T(8,128)(2,1)} fusion(bf16[128,512]{1,0:T(8,128)(2,1)} %param.10, pred[]{:T(512)S(6)} %lt.14), kind=kLoop, calls=%fused_computation | loop fusion | flops 65536 | bytes 262145 | tf_op jit(solution)/shard_map/jit(_where)/select_n | solution.py:212
  7.5 4.0 %pick_tiles.1.out_tiles = bf16[64,128,128]{2,1,0:T(8,128)(2,1)} custom-call(s32[64]{0:T(128)} %dynamic-slice_bitcast_fusion.cols_ref, bf16[128,8192]{1,0:T(8,128)(2,1)} %store_ref.1), custom_call_target="tpu_custom_call" | custom-call | tf_op jit(solution)/shard_map/pick_tiles/pallas_call | solution.py:27
  11.5 84.1 %level.1 = (bf16[128,512]{1,0:T(8,128)(2,1)}, bf16[8,64,512]{2,1,0:T(8,128)(2,1)}, f32[64,512]{1,0:T(8,128)}) custom-call(s32[8]{0:T(128)} %select_reduce_fusion.src_ref, bf16[64,128,128]{2,1,0:T(8,128)(2,1)} %pick_tiles.1.out_tiles, bf16[128,512]{1,0:T(8,128)(2,1)} %broadcast_select_fusion.l_ref, bf16[64,512]{1,0:T(8,128)(2,1)} %diag_ref.1, ...), custom_call_target="tpu_custom_call" | custom-call | tf_op jit(solution)/shard_map/level/pallas_call | solution.py:154
  95.6 1.8 %finish.1 = (bf16[128,512]{1,0:T(8,128)(2,1)}, f32[64,512]{1,0:T(8,128)}) custom-call(bf16[128,512]{1,0:T(8,128)(2,1)} %get-tuple-element.5.y_ref, bf16[8,64,512]{2,1,0:T(8,128)(2,1)} %get-tuple-element.6.parts_ref, f32[64,512]{1,0:T(8,128)} %get-tuple-element.7.base_ref), custom_call_target="tpu_custom_call" | custom-call | tf_op jit(solution)/shard_map/finish/pallas_call | solution.py:192
Async XLA Ops:
  0.6 0.7 copy-start

commit v3 on v2

v3 whole, which is shorter than its diff:
```python
import functools

import jax
import jax.numpy as jnp
from jax import lax
from jax.experimental import pallas as pl
from jax.experimental.pallas import tpu as pltpu
from jax.sharding import PartitionSpec as P

LANES = 128
MESH = pl.DeviceIdType.MESH
VMEM = pl.BlockSpec(memory_space=pltpu.VMEM)


ORDER = (3, 5, 2, 6, 1, 7, 4)


def pick_kernel(
    tile, patterns_ref, counts_ref, owner_ref, store_ref, l_ref,
    out_ref, src_ref, masked_ref, live_ref, sem,
):
    group, part = lax.axis_index("snode"), lax.axis_index("rows")
    majors, minors = out_ref.shape[:2]

    def start(i, carry):
        col = pl.multiple_of(patterns_ref[part, i] * tile, tile)
        pltpu.make_async_copy(
            store_ref.at[:, pl.ds(col, tile)], out_ref.at[i // minors, lax.rem(i, minors)], sem
        ).start()
        return carry

    lax.fori_loop(0, majors * minors, start, 0)
    slots = patterns_ref.shape[0]
    for k in range(slots):
        owner = owner_ref[patterns_ref[k, group]]
        src_ref[k] = owner
        src_ref[slots + k] = lax.rem(owner, minors) * majors + owner // minors
    live = (part < counts_ref[group]).astype(jnp.float32)
    keep = jnp.full(live_ref.shape, live, jnp.float32)
    live_ref[...] = keep
    loaded = l_ref[...]
    masked_ref[...] = jnp.where(keep > 0, loaded, jnp.zeros_like(loaded))
    pltpu.make_async_copy(out_ref, out_ref, sem).wait()


def pick_tiles(patterns, counts, owner, store, l_offdiag, side):
    tile = store.shape[0]
    smem = pl.BlockSpec(memory_space=pltpu.SMEM)
    return pl.pallas_call(
        functools.partial(pick_kernel, tile),
        out_shape=(
            jax.ShapeDtypeStruct((owner.shape[0] // side, side, tile, tile), store.dtype),
            jax.ShapeDtypeStruct((2 * patterns.shape[0],), jnp.int32),
            jax.ShapeDtypeStruct(l_offdiag.shape, l_offdiag.dtype),
            jax.ShapeDtypeStruct((1, l_offdiag.shape[1]), jnp.float32),
        ),
        in_specs=[smem] * 3 + [pl.BlockSpec(memory_space=pl.ANY), VMEM],
        out_specs=(VMEM, smem, VMEM, VMEM),
        scratch_shapes=[pltpu.SemaphoreType.DMA],
        name="pick_tiles",
    )(patterns, counts, owner, store, l_offdiag)


def level_kernel(
    n, src_ref, out_tiles, l_ref, diag_ref, live_ref,
    y_ref, parts_ref, base_ref,
    top_mid, low_mid, top_pool, low_pool, diag_all, u_all, stage, tiles, parts, wide, total,
    pool_send, pool_recv, row_send, row_recv, local_sem,
):
    snode, me = lax.axis_index("snode"), lax.axis_index("rows")
    majors, minors, tile, _ = out_tiles.shape
    half = tile // 2
    major, minor = snode // minors, lax.rem(snode, minors)

    barrier = pltpu.get_barrier_semaphore()
    for step in range(1, n):
        pl.semaphore_signal(
            barrier, inc=1, device_id=(snode, lax.rem(me + step, n)), device_id_type=MESH
        )
    for step in ORDER:
        for peer in (
            major * minors + lax.rem(minor + step, minors),
            lax.rem(major + step, majors) * minors + minor,
        ):
            pl.semaphore_signal(barrier, inc=1, device_id=(peer, me), device_id_type=MESH)
    pl.semaphore_wait(barrier, n - 1 + 2 * len(ORDER))

    def row_copies(phase, src_of, dst):
        copies = []
        for step in range(1, n):
            peer = lax.rem(me + step, n)
            copy = pltpu.make_async_remote_copy(
                src_ref=src_of(peer),
                dst_ref=dst.at[me],
                send_sem=row_send.at[phase, step - 1],
                recv_sem=row_recv.at[phase, step - 1],
                device_id=(snode, peer),
                device_id_type=MESH,
            )
            copy.start()
            copies.append(copy)
        return copies

    def pool_copies(phase, top_src, top_dst, low_src, low_dst):
        copies = []
        for step in ORDER:
            to_minor, to_major = lax.rem(minor + step, minors), lax.rem(major + step, majors)
            along_minor = (to_minor, (major * minors + to_minor, me))
            along_major = (to_major, (to_major * minors + minor, me))
            first, second = (along_minor, along_major) if phase == 0 else (along_major, along_minor)
            for lane, src, dst, (index, device) in (
                (2 * phase, top_src, top_dst, first),
                (2 * phase + 1, low_src, low_dst, second),
            ):
                copy = pltpu.make_async_remote_copy(
                    src_ref=src(index),
                    dst_ref=dst,
                    send_sem=pool_send.at[lane, step - 1],
                    recv_sem=pool_recv.at[lane, step - 1],
                    device_id=device,
                    device_id_type=MESH,
                )
                copy.start()
                copies.append(copy)
        return copies

    def local(slot, src, dst):
        copy = pltpu.make_async_copy(src, dst, local_sem.at[slot])
        copy.start()
        return copy

    top_out = lambda to: out_tiles.at[:, to, pl.ds(0, half)]
    low_out = lambda to: out_tiles.at[to, :, pl.ds(half, half)]
    diag_copies = row_copies(0, lambda peer: diag_ref, diag_all)
    first = pool_copies(0, top_out, top_mid.at[minor], low_out, low_mid.at[major])
    own_diag = local(0, diag_ref, diag_all.at[me])
    own_top = local(1, top_out(minor), top_mid.at[minor])
    own_low = local(2, low_out(major), low_mid.at[major])
    own_diag.wait()
    for copy in diag_copies:
        copy.wait()

    band, width = diag_ref.shape
    depth = l_ref.shape[0]
    piece = diag_all[...].reshape(width, width)
    u_all[me] = jnp.dot(l_ref[...], piece, preferred_element_type=jnp.float32).astype(u_all.dtype)
    per_block = LANES // band
    start = pl.multiple_of(me // per_block * LANES, LANES)
    columns = diag_all[:, :, pl.ds(start, LANES)].reshape(width, LANES)
    wide[...] = lax.dot_general(
        columns, piece, (((0,), (0,)), ((), ())), preferred_element_type=jnp.float32
    )
    row = pl.multiple_of(lax.rem(me, per_block) * band, band)
    base_ref[...] = wide[pl.ds(row, band), :]
    u_copies = row_copies(1, lambda peer: u_all.at[me], u_all)
    own_top.wait()
    own_low.wait()
    for copy in first:
        copy.wait()
    top_via = lambda to: top_mid.at[:, to]
    low_via = lambda to: low_mid.at[:, to]
    second = pool_copies(1, top_via, top_pool.at[major], low_via, low_pool.at[minor])
    end_top = local(3, top_via(major), top_pool.at[major])
    end_low = local(4, low_via(minor), low_pool.at[minor])
    for copy in u_copies:
        copy.wait()
    end_top.wait()
    end_low.wait()
    for copy in second:
        copy.wait()

    for k in range(n):
        top, low = src_ref[k], src_ref[n + k]
        stage[k, :half] = top_pool[top // minors, lax.rem(top, minors)]
        stage[k, half:] = low_pool[low // majors, lax.rem(low, majors)]
    tile_copies = row_copies(2, lambda peer: stage.at[peer], tiles)
    total[...] = jnp.dot(stage[me], u_all[me], preferred_element_type=jnp.float32)
    for step, copy in enumerate(tile_copies):
        copy.wait()
        origin = lax.rem(me + n - 1 - step, n)
        total[...] += jnp.dot(tiles[origin], u_all[origin], preferred_element_type=jnp.float32)
    y = (-(total[...] * live_ref[...])).astype(y_ref.dtype)
    part = lax.dot_general(
        u_all[me], y, (((0,), (0,)), ((), ())), preferred_element_type=jnp.float32
    )
    parts[...] = part.astype(parts.dtype).reshape(parts.shape)
    y_ref[...] = y
    part_copies = row_copies(3, lambda peer: parts.at[peer], parts_ref)
    local(5, parts.at[me], parts_ref.at[me]).wait()
    for copy in part_copies:
        copy.wait()


def level(outgoing, sources, masked_l, live, diag, n):
    majors, minors, tile, _ = outgoing.shape
    band, width = diag.shape
    bf16 = jnp.bfloat16
    return pl.pallas_call(
        functools.partial(level_kernel, n),
        out_shape=(
            jax.ShapeDtypeStruct((tile, width), bf16),
            jax.ShapeDtypeStruct((n, band, width), bf16),
            jax.ShapeDtypeStruct((band, width), jnp.float32),
        ),
        in_specs=[pl.BlockSpec(memory_space=pltpu.SMEM)] + [VMEM] * 4,
        out_specs=(VMEM,) * 3,
        scratch_shapes=[
            pltpu.VMEM((minors, majors, tile // 2, tile), bf16),
            pltpu.VMEM((majors, minors, tile // 2, tile), bf16),
            pltpu.VMEM((majors, minors, tile // 2, tile), bf16),
            pltpu.VMEM((minors, majors, tile // 2, tile), bf16),
            pltpu.VMEM((n, band, width), bf16),
            pltpu.VMEM((n, tile, width), bf16),
            pltpu.VMEM((n, tile, tile), bf16),
            pltpu.VMEM((n, tile, tile), bf16),
            pltpu.VMEM((n, band, width), bf16),
            pltpu.VMEM((LANES, width), jnp.float32),
            pltpu.VMEM((tile, width), jnp.float32),
            pltpu.SemaphoreType.DMA((4, len(ORDER))),
            pltpu.SemaphoreType.DMA((4, len(ORDER))),
            pltpu.SemaphoreType.DMA((4, n - 1)),
            pltpu.SemaphoreType.DMA((4, n - 1)),
            pltpu.SemaphoreType.DMA((6,)),
        ],
        compiler_params=pltpu.CompilerParams(collective_id=1, has_side_effects=True),
        name="level",
    )(sources, outgoing, masked_l, diag, live)


def finish_kernel(y_ref, parts_ref, base_ref, off_ref, diag_ref):
    off_ref[...] = y_ref[...]
    total = base_ref[...]
    for m in range(parts_ref.shape[0]):
        total -= parts_ref[m].astype(jnp.float32)
    diag_ref[...] = total


def finish(y, parts, base):
    return pl.pallas_call(
        finish_kernel,
        out_shape=(
            jax.ShapeDtypeStruct(y.shape, y.dtype),
            jax.ShapeDtypeStruct(base.shape, base.dtype),
        ),
        in_specs=[VMEM] * 3,
        out_specs=(VMEM, VMEM),
        name="finish",
    )(y, parts, base)


def per_device(n, side, anc_store, patterns, tile_counts, tile_owner, l_offdiag, diag_inverse):
    picked = pick_tiles(patterns.T, tile_counts, tile_owner, anc_store, l_offdiag, side)
    return finish(*level(*picked, diag_inverse, n))


def solution(mesh):
    in_specs = (
        P("snode", None),
        P(),
        P(),
        P(),
        P(("snode", "rows"), None),
        P(("snode", "rows"), None),
    )
    out_specs = (P(("snode", "rows"), None), P(("snode", "rows"), None))
    return jax.shard_map(
        functools.partial(per_device, mesh.shape["rows"], 8),
        mesh=mesh,
        in_specs=in_specs,
        out_specs=out_specs,
        check_vma=False,
    )
```

time: 97.8 us -> 89.2 us (0.912)
  local copies, waits for them, and re-layouts: 3.21 us -> 0 us
  other arithmetic: 2.98 us -> 0 us
  Pallas kernels: 89.9 us -> 88.3 us
    pallas_call x2, Pallas kernels: 88.1 us -> 86.5 us  [the longest x1 82.2 us: level(): pl.pallas_call(functools.partial(level_kernel, n), out_shape=(jax.ShapeDt...]
    select_n x1 -> x0, other arithmetic: 1.57 us -> none  [per_device(): masked_l = jnp.where(own_live, l_offdiag, jnp.zeros_like(l_offdiag))]
    dynamic_slice x2 -> x0, local copies, waits for them, and re-layouts: 1.42 us -> none  [the longest x1 1.24 us: per_device(): lax.dynamic_index_in_dim(tile_counts, group, 0, keepdims=False)]
    reduce_sum x1 -> x0, other arithmetic: 1.41 us -> none  [per_device(): sources = jnp.sum(jnp.where(hit, tile_owner[None, :], 0), axis=1)]
where the time goes in v3:
time: 89.2 us; the launch traced here: 89 us
  Pallas kernels  88.3 us (99%)
    pallas_call x1, Pallas kernels, level(): pl.pallas_call(functools.partial(level_kernel, n), out_shape=(jax.ShapeDt...  82.2 us
    pallas_call x1, Pallas kernels, pick_tiles(): pl.pallas_call(functools.partial(pick_kernel, tile), out_shape=(jax.Shape...  4.32 us
    pallas_call x1, Pallas kernels, finish(): pl.pallas_call(finish_kernel, out_shape=(jax.ShapeDtypeStruct(y.shape, y....  1.84 us

profile of v3, /device:TPU:1, one launch (start us, length us, event | category | flops | bytes accessed | tf_op | source)
XLA Modules:
  0.0 89.0 jit_solution(17881096182511661055)
XLA Ops:
  0.6 4.3 %pick_tiles.1 = (bf16[8,8,128,128]{3,2,1,0:T(8,128)(2,1)}, s32[16]{0:T(128)}, bf16[128,512]{1,0:T(8,128)(2,1)}, f32[1,512]{1,0:T(1,128)}) custom-call(s32[8,64]{1,0:T(8,128)} %bitcast.1, s32[64]{0:T(128)} %counts_ref.1, s32[64]{0:T(128)} %owner_ref.1, bf16[128,8192]{1,0:T(8,128)(2,1)} %store_ref.1, bf16[128,512]{1,0:T(8,128)(2,1)} %l_ref.1), custom_call_target="tpu_custom_call" | custom-call | tf_op jit(solution)/shard_map/pick_tiles/pallas_call | solution.py:49
  5.0 82.2 %level.1 = (bf16[128,512]{1,0:T(8,128)(2,1)}, bf16[8,64,512]{2,1,0:T(8,128)(2,1)}, f32[64,512]{1,0:T(8,128)}) custom-call(s32[16]{0:T(128)} %get-tuple-element.9.src_ref, bf16[8,8,128,128]{3,2,1,0:T(8,128)(2,1)} %get-tuple-element.10.out_tiles, bf16[128,512]{1,0:T(8,128)(2,1)} %get-tuple-element.11.l_ref, bf16[64,512]{1,0:T(8,128)(2,1)} %diag_ref.1, ...), custom_call_target="tpu_custom_call" | custom-call | tf_op jit(solution)/shard_map/level/pallas_call | solution.py:198
  87.1 1.8 %finish.1 = (bf16[128,512]{1,0:T(8,128)(2,1)}, f32[64,512]{1,0:T(8,128)}) custom-call(bf16[128,512]{1,0:T(8,128)(2,1)} %get-tuple-element.13.y_ref, bf16[8,64,512]{2,1,0:T(8,128)(2,1)} %get-tuple-element.14.parts_ref, f32[64,512]{1,0:T(8,128)} %get-tuple-element.15.base_ref), custom_call_target="tpu_custom_call" | custom-call | tf_op jit(solution)/shard_map/finish/pallas_call | solution.py:239

commit v4 on v3

--- a/solution.py
+++ b/solution.py
@@ -12,7 +12,8 @@
 VMEM = pl.BlockSpec(memory_space=pltpu.VMEM)
 
 
-ORDER = (3, 5, 2, 6, 1, 7, 4)
+ORDER = (1, 7, 2, 6, 3, 5, 4)
+PARTS = 2
 
 
 def pick_kernel(
@@ -31,10 +32,16 @@
 
     lax.fori_loop(0, majors * minors, start, 0)
     slots = patterns_ref.shape[0]
-    for k in range(slots):
-        owner = owner_ref[patterns_ref[k, group]]
-        src_ref[k] = owner
-        src_ref[slots + k] = lax.rem(owner, minors) * majors + owner // minors
+
+    def look_up(i, carry):
+        top = i * minors + lax.rem(group, minors)
+        low = group // minors * minors + i
+        for k in range(slots):
+            src_ref[0, i * slots + k] = owner_ref[patterns_ref[k, top]]
+            src_ref[1, i * slots + k] = owner_ref[patterns_ref[k, low]]
+        return carry
+
+    lax.fori_loop(0, majors, look_up, 0)
     live = (part < counts_ref[group]).astype(jnp.float32)
     keep = jnp.full(live_ref.shape, live, jnp.float32)
     live_ref[...] = keep
@@ -50,7 +57,7 @@
         functools.partial(pick_kernel, tile),
         out_shape=(
             jax.ShapeDtypeStruct((owner.shape[0] // side, side, tile, tile), store.dtype),
-            jax.ShapeDtypeStruct((2 * patterns.shape[0],), jnp.int32),
+            jax.ShapeDtypeStruct((2, side * patterns.shape[0]), jnp.int32),
             jax.ShapeDtypeStruct(l_offdiag.shape, l_offdiag.dtype),
             jax.ShapeDtypeStruct((1, l_offdiag.shape[1]), jnp.float32),
         ),
@@ -64,8 +71,8 @@
 def level_kernel(
     n, src_ref, out_tiles, l_ref, diag_ref, live_ref,
     y_ref, parts_ref, base_ref,
-    top_mid, low_mid, top_pool, low_pool, diag_all, u_all, stage, tiles, parts, wide, total,
-    pool_send, pool_recv, row_send, row_recv, local_sem,
+    top_mid, low_mid, held, sent, diag_all, u_all, stage, tiles, parts, wide, total,
+    pool_send, pool_recv, chain_send, chain_recv, row_send, row_recv, local_sem,
 ):
     snode, me = lax.axis_index("snode"), lax.axis_index("rows")
     majors, minors, tile, _ = out_tiles.shape
@@ -101,19 +108,16 @@
             copies.append(copy)
         return copies
 
-    def pool_copies(phase, top_src, top_dst, low_src, low_dst):
+    def pool_copies():
         copies = []
         for step in ORDER:
             to_minor, to_major = lax.rem(minor + step, minors), lax.rem(major + step, majors)
-            along_minor = (to_minor, (major * minors + to_minor, me))
-            along_major = (to_major, (to_major * minors + minor, me))
-            first, second = (along_minor, along_major) if phase == 0 else (along_major, along_minor)
-            for lane, src, dst, (index, device) in (
-                (2 * phase, top_src, top_dst, first),
-                (2 * phase + 1, low_src, low_dst, second),
+            for lane, src, dst, device in (
+                (0, top_out(to_minor), top_mid.at[minor], line(0, to_minor)),
+                (1, low_out(to_major), low_mid.at[major], line(1, to_major)),
             ):
                 copy = pltpu.make_async_remote_copy(
-                    src_ref=src(index),
+                    src_ref=src,
                     dst_ref=dst,
                     send_sem=pool_send.at[lane, step - 1],
                     recv_sem=pool_recv.at[lane, step - 1],
@@ -124,6 +128,46 @@
                 copies.append(copy)
         return copies
 
+    def line(lane, index):
+        if lane == 0:
+            return (major * minors + index, me)
+        return (index * minors + minor, me)
+
+    sign = 1 - 2 * lax.rem(me, 2)
+
+    def own_part_of(lane, target, k):
+        owner = src_ref[lane, target * n + k]
+        if lane == 0:
+            place, entry = owner // minors, lax.rem(owner, minors)
+            return place, top_mid[entry, target]
+        place, entry = lax.rem(owner, minors), owner // minors
+        return place, low_mid[entry, target]
+
+    def chain_step(lane, way, step, part, before):
+        here, size = (major, majors) if lane == 0 else (minor, minors)
+        length = size // 2 - way
+        toward = sign if way else -sign
+        target = lax.rem(here + toward * (length - step) + size, size)
+        slots = range(part * n // PARTS, (part + 1) * n // PARTS)
+        if before is not None:
+            before.wait_recv()
+        for k in slots:
+            place, mine = own_part_of(lane, target, k)
+            if before is not None:
+                mine = jnp.where(place == here, mine, held[lane, way, step - 1, k])
+            sent[lane, way, step, k] = mine
+        span = pl.ds(part * n // PARTS, n // PARTS)
+        copy = pltpu.make_async_remote_copy(
+            src_ref=sent.at[lane, way, step, span],
+            dst_ref=held.at[lane, way, step, span],
+            send_sem=chain_send.at[lane, way, step, part],
+            recv_sem=chain_recv.at[lane, way, step, part],
+            device_id=line(1 - lane, lax.rem(here + toward + size, size)),
+            device_id_type=MESH,
+        )
+        copy.start()
+        return copy
+
     def local(slot, src, dst):
         copy = pltpu.make_async_copy(src, dst, local_sem.at[slot])
         copy.start()
@@ -132,7 +176,7 @@
     top_out = lambda to: out_tiles.at[:, to, pl.ds(0, half)]
     low_out = lambda to: out_tiles.at[to, :, pl.ds(half, half)]
     diag_copies = row_copies(0, lambda peer: diag_ref, diag_all)
-    first = pool_copies(0, top_out, top_mid.at[minor], low_out, low_mid.at[major])
+    first = pool_copies()
     own_diag = local(0, diag_ref, diag_all.at[me])
     own_top = local(1, top_out(minor), top_mid.at[minor])
     own_low = local(2, low_out(major), low_mid.at[major])
@@ -157,22 +201,32 @@
     own_low.wait()
     for copy in first:
         copy.wait()
-    top_via = lambda to: top_mid.at[:, to]
-    low_via = lambda to: low_mid.at[:, to]
-    second = pool_copies(1, top_via, top_pool.at[major], low_via, low_pool.at[minor])
-    end_top = local(3, top_via(major), top_pool.at[major])
-    end_low = local(4, low_via(minor), low_pool.at[minor])
+    last, everything = {}, []
+    for step in range(max(majors, minors) // 2):
+        for part in range(PARTS):
+            for way in (0, 1):
+                for lane in (0, 1):
+                    if step < (majors, minors)[lane] // 2 - way:
+                        key = (lane, way, part)
+                        last[key] = chain_step(lane, way, step, part, last.get(key))
+                        everything.append(last[key])
     for copy in u_copies:
         copy.wait()
-    end_top.wait()
-    end_low.wait()
-    for copy in second:
-        copy.wait()
-
-    for k in range(n):
-        top, low = src_ref[k], src_ref[n + k]
-        stage[k, :half] = top_pool[top // minors, lax.rem(top, minors)]
-        stage[k, half:] = low_pool[low // majors, lax.rem(low, majors)]
+    for copy in last.values():
+        copy.wait_recv()
+    for lane in (0, 1):
+        here, size = (major, majors) if lane == 0 else (minor, minors)
+        for k in range(n):
+            place, mine = own_part_of(lane, here, k)
+            away = lax.rem((place - here) * sign + size, size)
+            other = jnp.where(
+                away <= size // 2,
+                held[lane, 0, size // 2 - 1, k],
+                held[lane, 1, size // 2 - 2, k],
+            )
+            stage[k, lane * half : (lane + 1) * half] = jnp.where(away == 0, mine, other)
+    for copy in everything:
+        copy.wait_send()
     tile_copies = row_copies(2, lambda peer: stage.at[peer], tiles)
     total[...] = jnp.dot(stage[me], u_all[me], preferred_element_type=jnp.float32)
     for step, copy in enumerate(tile_copies):
@@ -207,8 +261,8 @@
         scratch_shapes=[
             pltpu.VMEM((minors, majors, tile // 2, tile), bf16),
             pltpu.VMEM((majors, minors, tile // 2, tile), bf16),
-            pltpu.VMEM((majors, minors, tile // 2, tile), bf16),
-            pltpu.VMEM((minors, majors, tile // 2, tile), bf16),
+            pltpu.VMEM((2, 2, max(majors, minors) // 2, n, tile // 2, tile), bf16),
+            pltpu.VMEM((2, 2, max(majors, minors) // 2, n, tile // 2, tile), bf16),
             pltpu.VMEM((n, band, width), bf16),
             pltpu.VMEM((n, tile, width), bf16),
             pltpu.VMEM((n, tile, tile), bf16),
@@ -216,8 +270,10 @@
             pltpu.VMEM((n, band, width), bf16),
             pltpu.VMEM((LANES, width), jnp.float32),
             pltpu.VMEM((tile, width), jnp.float32),
-            pltpu.SemaphoreType.DMA((4, len(ORDER))),
-            pltpu.SemaphoreType.DMA((4, len(ORDER))),
+            pltpu.SemaphoreType.DMA((2, len(ORDER))),
+            pltpu.SemaphoreType.DMA((2, len(ORDER))),
+            pltpu.SemaphoreType.DMA((2, 2, max(majors, minors) // 2, PARTS)),
+            pltpu.SemaphoreType.DMA((2, 2, max(majors, minors) // 2, PARTS)),
             pltpu.SemaphoreType.DMA((4, n - 1)),
             pltpu.SemaphoreType.DMA((4, n - 1)),
             pltpu.SemaphoreType.DMA((6,)),

time: 89.2 us -> 80.5 us (0.902)
  Pallas kernels: 88.3 us -> 79.6 us
    pallas_call x1, Pallas kernels: 82.2 us -> 73.3 us  [level(): pl.pallas_call(functools.partial(level_kernel, n), out_shape=(jax.ShapeDt...]
where the time goes in v4:
time: 80.5 us; the launch traced here: 80.2 us
  Pallas kernels  79.6 us (99%)
    pallas_call x1, Pallas kernels, level(): pl.pallas_call(functools.partial(level_kernel, n), out_shape=(jax.ShapeDt...  73.3 us
    pallas_call x1, Pallas kernels, pick_tiles(): pl.pallas_call(functools.partial(pick_kernel, tile), out_shape=(jax.Shape...  4.49 us
    pallas_call x1, Pallas kernels, finish(): pl.pallas_call(finish_kernel, out_shape=(jax.ShapeDtypeStruct(y.shape, y....  1.84 us

profile of v4, /device:TPU:1, one launch (start us, length us, event | category | flops | bytes accessed | tf_op | source)
XLA Modules:
  0.0 80.2 jit_solution(2081064599898004265)
XLA Ops:
  0.6 4.5 %pick_tiles.1 = (bf16[8,8,128,128]{3,2,1,0:T(8,128)(2,1)}, s32[2,64]{1,0:T(2,128)}, bf16[128,512]{1,0:T(8,128)(2,1)}, f32[1,512]{1,0:T(1,128)}) custom-call(s32[8,64]{1,0:T(8,128)} %bitcast.1, s32[64]{0:T(128)} %counts_ref.1, s32[64]{0:T(128)} %owner_ref.1, bf16[128,8192]{1,0:T(8,128)(2,1)} %store_ref.1, bf16[128,512]{1,0:T(8,128)(2,1)} %l_ref.1), custom_call_target="tpu_custom_call" | custom-call | tf_op jit(solution)/shard_map/pick_tiles/pallas_call | solution.py:56
  5.1 73.3 %level.1 = (bf16[128,512]{1,0:T(8,128)(2,1)}, bf16[8,64,512]{2,1,0:T(8,128)(2,1)}, f32[64,512]{1,0:T(8,128)}) custom-call(s32[2,64]{1,0:T(2,128)} %get-tuple-element.9.src_ref, bf16[8,8,128,128]{3,2,1,0:T(8,128)(2,1)} %get-tuple-element.10.out_tiles, bf16[128,512]{1,0:T(8,128)(2,1)} %get-tuple-element.11.l_ref, bf16[64,512]{1,0:T(8,128)(2,1)} %diag_ref.1, ...), custom_call_target="tpu_custom_call" | custom-call | tf_op jit(solution)/shard_map/level/pallas_call | solution.py:252
  78.4 1.8 %finish.1 = (bf16[128,512]{1,0:T(8,128)(2,1)}, f32[64,512]{1,0:T(8,128)}) custom-call(bf16[128,512]{1,0:T(8,128)(2,1)} %get-tuple-element.13.y_ref, bf16[8,64,512]{2,1,0:T(8,128)(2,1)} %get-tuple-element.14.parts_ref, f32[64,512]{1,0:T(8,128)} %get-tuple-element.15.base_ref), custom_call_target="tpu_custom_call" | custom-call | tf_op jit(solution)/shard_map/finish/pallas_call | solution.py:295

commit v5 on v4

--- a/solution.py
+++ b/solution.py
@@ -111,7 +111,8 @@
     def pool_copies():
         copies = []
         for step in ORDER:
-            to_minor, to_major = lax.rem(minor + step, minors), lax.rem(major + step, majors)
+            to_minor = lax.rem(minor + sign * step + minors, minors)
+            to_major = lax.rem(major + sign * step + majors, majors)
             for lane, src, dst, device in (
                 (0, top_out(to_minor), top_mid.at[minor], line(0, to_minor)),
                 (1, low_out(to_major), low_mid.at[major], line(1, to_major)),
@@ -200,7 +201,7 @@
     own_top.wait()
     own_low.wait()
     for copy in first:
-        copy.wait()
+        copy.wait_recv()
     last, everything = {}, []
     for step in range(max(majors, minors) // 2):
         for part in range(PARTS):
@@ -225,8 +226,6 @@
                 held[lane, 1, size // 2 - 2, k],
             )
             stage[k, lane * half : (lane + 1) * half] = jnp.where(away == 0, mine, other)
-    for copy in everything:
-        copy.wait_send()
     tile_copies = row_copies(2, lambda peer: stage.at[peer], tiles)
     total[...] = jnp.dot(stage[me], u_all[me], preferred_element_type=jnp.float32)
     for step, copy in enumerate(tile_copies):
@@ -242,7 +241,9 @@
     part_copies = row_copies(3, lambda peer: parts.at[peer], parts_ref)
     local(5, parts.at[me], parts_ref.at[me]).wait()
     for copy in part_copies:
-        copy.wait()
+        copy.wait_recv()
+    for copy in first + everything + part_copies:
+        copy.wait_send()
 
 
 def level(outgoing, sources, masked_l, live, diag, n):
@@ -256,7 +257,11 @@
             jax.ShapeDtypeStruct((n, band, width), bf16),
             jax.ShapeDtypeStruct((band, width), jnp.float32),
         ),
-        in_specs=[pl.BlockSpec(memory_space=pltpu.SMEM)] + [VMEM] * 4,
+        in_specs=[
+            pl.BlockSpec(memory_space=pltpu.SMEM),
+            pl.BlockSpec(memory_space=pl.ANY),
+        ]
+        + [VMEM] * 3,
         out_specs=(VMEM,) * 3,
         scratch_shapes=[
             pltpu.VMEM((minors, majors, tile // 2, tile), bf16),

time: 80.5 us -> 80.1 us (level)
  no operation moved by 1% of the time
where the time goes in v5:
time: 80.1 us; the launch traced here: 79.8 us
  Pallas kernels  79.2 us (99%)
    pallas_call x1, Pallas kernels, level(): pl.pallas_call(functools.partial(level_kernel, n), out_shape=(jax.ShapeDt...  72.8 us
    pallas_call x1, Pallas kernels, pick_tiles(): pl.pallas_call(functools.partial(pick_kernel, tile), out_shape=(jax.Shape...  4.54 us
    pallas_call x1, Pallas kernels, finish(): pl.pallas_call(finish_kernel, out_shape=(jax.ShapeDtypeStruct(y.shape, y....  1.84 us

profile of v5, /device:TPU:1, one launch (start us, length us, event | category | flops | bytes accessed | tf_op | source)
XLA Modules:
  0.0 79.8 jit_solution(9048163428363052681)
XLA Ops:
  0.6 4.5 %pick_tiles.1 = (bf16[8,8,128,128]{3,2,1,0:T(8,128)(2,1)}, s32[2,64]{1,0:T(2,128)}, bf16[128,512]{1,0:T(8,128)(2,1)}, f32[1,512]{1,0:T(1,128)}) custom-call(s32[8,64]{1,0:T(8,128)} %bitcast.1, s32[64]{0:T(128)} %counts_ref.1, s32[64]{0:T(128)} %owner_ref.1, bf16[128,8192]{1,0:T(8,128)(2,1)} %store_ref.1, bf16[128,512]{1,0:T(8,128)(2,1)} %l_ref.1), custom_call_target="tpu_custom_call" | custom-call | tf_op jit(solution)/shard_map/pick_tiles/pallas_call | solution.py:56
  5.2 72.8 %level.1 = (bf16[128,512]{1,0:T(8,128)(2,1)}, bf16[8,64,512]{2,1,0:T(8,128)(2,1)}, f32[64,512]{1,0:T(8,128)}) custom-call(s32[2,64]{1,0:T(2,128)} %get-tuple-element.9.src_ref, bf16[8,8,128,128]{3,2,1,0:T(8,128)(2,1)} %get-tuple-element.10.out_tiles, bf16[128,512]{1,0:T(8,128)(2,1)} %get-tuple-element.11.l_ref, bf16[64,512]{1,0:T(8,128)(2,1)} %diag_ref.1, ...), custom_call_target="tpu_custom_call" | custom-call | tf_op jit(solution)/shard_map/level/pallas_call | solution.py:253
  78.0 1.8 %finish.1 = (bf16[128,512]{1,0:T(8,128)(2,1)}, f32[64,512]{1,0:T(8,128)}) custom-call(bf16[128,512]{1,0:T(8,128)(2,1)} %get-tuple-element.13.y_ref, bf16[8,64,512]{2,1,0:T(8,128)(2,1)} %get-tuple-element.14.parts_ref, f32[64,512]{1,0:T(8,128)} %get-tuple-element.15.base_ref), custom_call_target="tpu_custom_call" | custom-call | tf_op jit(solution)/shard_map/finish/pallas_call | solution.py:300

commit v6 on v5

--- a/solution.py
+++ b/solution.py
@@ -92,9 +92,11 @@
             pl.semaphore_signal(barrier, inc=1, device_id=(peer, me), device_id_type=MESH)
     pl.semaphore_wait(barrier, n - 1 + 2 * len(ORDER))
 
+    far_first = sorted(range(1, n), key=lambda step: (abs(step - n // 2), step))
+
     def row_copies(phase, src_of, dst):
         copies = []
-        for step in range(1, n):
+        for step in far_first:
             peer = lax.rem(me + step, n)
             copy = pltpu.make_async_remote_copy(
                 src_ref=src_of(peer),
@@ -228,9 +230,9 @@
             stage[k, lane * half : (lane + 1) * half] = jnp.where(away == 0, mine, other)
     tile_copies = row_copies(2, lambda peer: stage.at[peer], tiles)
     total[...] = jnp.dot(stage[me], u_all[me], preferred_element_type=jnp.float32)
-    for step, copy in enumerate(tile_copies):
+    for step, copy in reversed(list(zip(far_first, tile_copies))):
         copy.wait()
-        origin = lax.rem(me + n - 1 - step, n)
+        origin = lax.rem(me + n - step, n)
         total[...] += jnp.dot(tiles[origin], u_all[origin], preferred_element_type=jnp.float32)
     y = (-(total[...] * live_ref[...])).astype(y_ref.dtype)
     part = lax.dot_general(

time: 80.1 us -> 79.3 us (0.990)
  no operation moved by 1% of the time
where the time goes in v6:
time: 79.3 us; the launch traced here: 79 us
  Pallas kernels  78.4 us (99%)
    pallas_call x1, Pallas kernels, level(): pl.pallas_call(functools.partial(level_kernel, n), out_shape=(jax.ShapeDt...  72 us
    pallas_call x1, Pallas kernels, pick_tiles(): pl.pallas_call(functools.partial(pick_kernel, tile), out_shape=(jax.Shape...  4.51 us
    pallas_call x1, Pallas kernels, finish(): pl.pallas_call(finish_kernel, out_shape=(jax.ShapeDtypeStruct(y.shape, y....  1.84 us

profile of v6, /device:TPU:1, one launch (start us, length us, event | category | flops | bytes accessed | tf_op | source)
XLA Modules:
  0.0 79.0 jit_solution(1664685220633572778)
XLA Ops:
  0.6 4.5 %pick_tiles.1 = (bf16[8,8,128,128]{3,2,1,0:T(8,128)(2,1)}, s32[2,64]{1,0:T(2,128)}, bf16[128,512]{1,0:T(8,128)(2,1)}, f32[1,512]{1,0:T(1,128)}) custom-call(s32[8,64]{1,0:T(8,128)} %bitcast.1, s32[64]{0:T(128)} %counts_ref.1, s32[64]{0:T(128)} %owner_ref.1, bf16[128,8192]{1,0:T(8,128)(2,1)} %store_ref.1, bf16[128,512]{1,0:T(8,128)(2,1)} %l_ref.1), custom_call_target="tpu_custom_call" | custom-call | tf_op jit(solution)/shard_map/pick_tiles/pallas_call | solution.py:56
  5.1 72.0 %level.1 = (bf16[128,512]{1,0:T(8,128)(2,1)}, bf16[8,64,512]{2,1,0:T(8,128)(2,1)}, f32[64,512]{1,0:T(8,128)}) custom-call(s32[2,64]{1,0:T(2,128)} %get-tuple-element.9.src_ref, bf16[8,8,128,128]{3,2,1,0:T(8,128)(2,1)} %get-tuple-element.10.out_tiles, bf16[128,512]{1,0:T(8,128)(2,1)} %get-tuple-element.11.l_ref, bf16[64,512]{1,0:T(8,128)(2,1)} %diag_ref.1, ...), custom_call_target="tpu_custom_call" | custom-call | tf_op jit(solution)/shard_map/level/pallas_call | solution.py:255
  77.2 1.8 %finish.1 = (bf16[128,512]{1,0:T(8,128)(2,1)}, f32[64,512]{1,0:T(8,128)}) custom-call(bf16[128,512]{1,0:T(8,128)(2,1)} %get-tuple-element.13.y_ref, bf16[8,64,512]{2,1,0:T(8,128)(2,1)} %get-tuple-element.14.parts_ref, f32[64,512]{1,0:T(8,128)} %get-tuple-element.15.base_ref), custom_call_target="tpu_custom_call" | custom-call | tf_op jit(solution)/shard_map/finish/pallas_call | solution.py:302
